TPU v7x, 32 devices: a whole 2x2x4 slice. The times are simulated.
32 devices in a mesh: virt: 8 (over y, x, core), occ: 4 (over z).
Axes of the slice: x: 2, y: 2, z: 4, core: 2. Of those that a mesh axis runs over, the one named last changes fastest.
Arguments:
- amplitudes: bfloat16 [512, 4096], P('occ', 'virt'), may hold values from -6 to 6
- integrals: bfloat16 [1024, 16384], P(None, 'virt'), may hold values from -0.1875 to 0.1875
- panel_owner: int32 [4, 2], P('occ'), may hold values from 0 to 7, as said below
- inter: bfloat16 [8192, 8192], P('occ', 'virt'), may hold values from -0.125 to 0.125
- dest: int32 [4, 8, 16], P('occ', 'virt'), may hold values from 0 to 3, as said below
- screen: int32 [4, 8, 16], P('occ', 'virt'), may hold values from 0 to 1
Outputs:
- contracted: bfloat16 [512, 8192], P('occ', 'virt')
Inputs may be any that keep to these rules, and one draw needn't show every extreme that they name: `panel_owner`: in each row the 2 entries are distinct. `dest`: among the subtiles of one device that screen marks 1, no two name the same owner.
All inputs are finite; a program needn't handle non-finite values.
Results may differ from a plain program's by a relative error of at most 0.0055.
Values may be sent and summed in bfloat16 or wider, within the bound.
A program may use at most 64 MiB of HBM per device.

v0:
```python
import jax
import jax.numpy as jnp
from jax import lax
from jax.sharding import PartitionSpec as P

SROWS = 32


def on_device(amplitudes, integrals, panel_owner, inter, dest, screen):
    op_rows = amplitudes.shape[0]
    tile = amplitudes.shape[1]
    cols = integrals.shape[1]
    steps = panel_owner.shape[1]
    n_sub = dest.shape[2]
    n_occ = lax.axis_size("occ")
    half_splits = op_rows // SROWS
    col_tiles = cols // tile
    every = lax.all_gather(amplitudes[None], "virt", axis=0, tiled=True)
    chosen_entries = jnp.take(every, panel_owner[0], axis=0)
    chosen_entries = chosen_entries.transpose(1, 0, 2).reshape(op_rows, steps * tile)
    accum = jnp.dot(chosen_entries, integrals, preferred_element_type=jnp.float32)
    ladder = accum.astype(jnp.bfloat16)
    subtiles = (
        ladder.reshape(half_splits, SROWS, col_tiles, tile)
        .transpose(0, 2, 1, 3)
        .reshape(n_sub, SROWS, tile)
    )
    owners = jnp.arange(n_occ, dtype=jnp.int32)
    labels = jnp.arange(1, n_sub + 1, dtype=jnp.int32)
    routing = (dest[0, 0][None, :] == owners[:, None]) & (screen[0, 0][None, :] == 1)
    outgoing = jnp.einsum(
        "os,srt->ort", routing.astype(jnp.bfloat16), subtiles, preferred_element_type=jnp.float32
    ).astype(jnp.bfloat16)
    output_marker = jnp.sum(routing.astype(jnp.int32) * labels[None, :], axis=1).astype(
        jnp.bfloat16
    )[:, None]
    arriving_tiles, tag_in = (
        lax.all_to_all(outgoing, "occ", split_axis=0, concat_axis=0, tiled=True),
        lax.all_to_all(output_marker, "occ", split_axis=0, concat_axis=0, tiled=True),
    )
    choose_surviving = tag_in.astype(jnp.float32) == labels[None, :].astype(jnp.float32)
    summed = jnp.einsum(
        "ez,ead->zad",
        choose_surviving.astype(jnp.bfloat16),
        arriving_tiles,
        preferred_element_type=jnp.float32,
    )
    gathered = summed.astype(jnp.bfloat16)
    left = (
        gathered.reshape(half_splits, col_tiles, SROWS, tile)
        .transpose(0, 2, 1, 3)
        .reshape(op_rows, cols)
    )
    return jnp.dot(left, inter, preferred_element_type=jnp.float32).astype(jnp.bfloat16)


def solution(mesh):
    return jax.shard_map(
        on_device,
        mesh=mesh,
        in_specs=(
            P("occ", "virt"),
            P(None, "virt"),
            P("occ", None),
            P("occ", "virt"),
            P("occ", "virt", None),
            P("occ", "virt", None),
        ),
        out_specs=P("occ", "virt"),
        check_vma=False,
    )
```

profile of v0, /device:TPU:0, one launch (start us, length us, event | category | flops | bytes accessed | tf_op | source)
XLA Modules:
  0.0 64.2 jit_solution(17440745688563391463)
XLA Ops:
  6.5 0.7 %all-gather.3.cloned.1.call-update = ((bf16[128,512]{1,0:T(8,128)(2,1)}), bf16[1024,512]{1,0:T(8,128)(2,1)}) async-update(((), (), s32[]{:S(2)}) %all-gather.3.cloned.1.call-start, bf16[128,512]{1,0:T(8,128)(2,1)} %param.6) | async-update | bytes 1310744
  7.3 0.7 %compare_bitcast_fusion = pred[16]{0:T(512)(128)(4,1)S(1)} fusion(s32[1,1,16]{2,1,0:T(1,128)} %param.11), kind=kLoop, calls=%fused_computation.19 | loop fusion | flops 16 | bytes 80 | tf_op jit(solution)/shard_map/eq | solution.py:30
  7.9 0.8 %select_reduce_fusion = s32[4]{0:T(128)S(1)} fusion(s32[16]{0:T(128)S(1)} %iota_add_fusion, s32[16]{0:T(128)} %bitcast.39, pred[16]{0:T(512)(128)(4,1)S(1)} %compare_bitcast_fusion), kind=kLoop, calls=%fused_computation.12 | loop fusion | flops 252 | bytes 160 | tf_op jit(solution)/shard_map/reduce_sum | solution.py:34
  8.7 0.7 %copy.20 = bf16[4,1,1]{2,1,0:T(2,128)(2,1)} copy(bf16[4,1,1]{0,2,1:T(2,128)(2,1)S(1)} %convert_bitcast_fusion) | data formatting | bytes 16 | tf_op jit(solution)/shard_map/convert_element_type | solution.py:34
  9.4 6.3 %all-to-all-start = ((bf16[4,1,1]{2,1,0:T(2,128)(2,1)}), bf16[4,1,1]{2,1,0:T(2,128)(2,1)S(1)}, u32[]{:S(2)}, u32[]{:S(2)}) async-start(bf16[4,1,1]{2,1,0:T(2,128)(2,1)} %copy.20), calls=%async_computation | async-start | bytes 4096 | tf_op jit(solution)/shard_map/all_to_all | solution.py:39
  15.7 0.7 %fusion.11 = s32[2]{0:T(128)S(1)} fusion(s32[1,2]{1,0:T(1,128)} %param.8), kind=kLoop, calls=%fused_computation.24 | loop fusion | flops 6 | bytes 16 | tf_op jit(solution)/shard_map/jit(_take)/jit(_where)/select_n | solution.py:19
  16.4 0.7 %compare_and_fusion = pred[2]{0:T(512)(128)(4,1)S(1)} fusion(s32[1,2]{1,0:T(1,128)} %param.8), kind=kLoop, calls=%fused_computation.17 | loop fusion | flops 12 | bytes 10 | tf_op jit(solution)/shard_map/jit(_take)/and | solution.py:19
  17.1 18.3 %all-gather.3.cloned.1.call-done = bf16[1024,512]{1,0:T(8,128)(2,1)} async-done(((bf16[128,512]{1,0:T(8,128)(2,1)}), bf16[1024,512]{1,0:T(8,128)(2,1)}) %all-gather.3.cloned.1.call-update) | async-done | bytes 1048592 | tf_op jit(solution)/shard_map/all_gather | solution.py:18
  35.3 1.8 %gather_fusion = bf16[2,128,512]{2,1,0:T(8,128)(2,1)S(1)} fusion(bf16[8,128,512]{2,1,0:T(8,128)(2,1)} %bitcast.38, s32[1024]{0:T(1024)S(1)} %pad_clamp_fusion), kind=kCustom, calls=%fused_computation | custom fusion | bytes 524296 | tf_op jit(solution)/shard_map/jit(_take)/gather | solution.py:19
  37.2 0.1 select_bitcast_fusion
  37.2 0.2 copy.21
  37.4 2.9 %convolution_convert_fusion = bf16[128,2048]{1,0:T(8,128)(2,1)S(1)} fusion(bf16[128,1024]{0,1:T(8,128)(2,1)S(1)} %bitcast.37, bf16[1024,2048]{1,0:T(8,128)(2,1)} %param.7), kind=kOutput, calls=%fused_computation.1 | convolution fusion | flops 537133056 | bytes 4980736 | tf_op jit(solution)/shard_map/dot_general | solution.py:21
  40.4 0.4 reshape.88
  40.7 0.1 copy.22
  40.9 0.4 convolution_convert_fusion.3
  41.3 0.7 %copy.24 = bf16[4,32,512]{2,1,0:T(8,128)(2,1)} copy(bf16[4,32,512]{2,0,1:T(4,128)(2,1)S(1)} %convolution_convert_fusion.3) | data formatting | bytes 262144 | tf_op jit(solution)/shard_map/convert_element_type | solution.py:33
  41.9 4.6 %all-to-all-start.1 = ((bf16[4,32,512]{2,1,0:T(8,128)(2,1)}), bf16[4,32,512]{2,1,0:T(8,128)(2,1)S(1)}, u32[]{:S(2)}, u32[]{:S(2)}) async-start(bf16[4,32,512]{2,1,0:T(8,128)(2,1)} %copy.24), calls=%async_computation.1 | async-start | bytes 262144 | tf_op jit(solution)/shard_map/all_to_all | solution.py:38
  46.6 0.1 convert_reduce_fusion
  46.7 6.2 %all-to-all-done.1 = bf16[4,32,512]{2,1,0:T(8,128)(2,1)S(1)} async-done(((bf16[4,32,512]{2,1,0:T(8,128)(2,1)}), bf16[4,32,512]{2,1,0:T(8,128)(2,1)S(1)}, u32[]{:S(2)}, u32[]{:S(2)}) %all-to-all-start.1) | async-done | bytes 131104 | tf_op jit(solution)/shard_map/all_to_all | solution.py:38
  52.8 0.5 convolution_convert_fusion.1
  53.3 0.1 reshape.90
  53.4 0.2 copy.26
  53.6 0.1 copy.27
  53.7 3.7 %convolution_convert_fusion.2 = bf16[128,1024]{1,0:T(8,128)(2,1)} fusion(bf16[128,2048]{1,0:T(8,128)(2,1)S(1)} %bitcast.34, bf16[2048,1024]{1,0:T(8,128)(2,1)} %param.9), kind=kOutput, calls=%fused_computation.3 | convolution fusion | flops 537001984 | bytes 4980736 | tf_op jit(solution)/shard_map/dot_general | solution.py:54
  (8 shorter events, 0.0 us)
Async XLA Ops:
  6.5 28.8 %all-gather.3.cloned.1.call-start = ((), (), s32[]{:S(2)}) async-start(), calls=%async_computation.2 | async-start | bytes 1179648 | tf_op jit(solution)/shard_map/all_gather | solution.py:18
  9.4 32.5 %all-to-all-start = ((bf16[4,1,1]{2,1,0:T(2,128)(2,1)}), bf16[4,1,1]{2,1,0:T(2,128)(2,1)S(1)}, u32[]{:S(2)}, u32[]{:S(2)}) async-start(bf16[4,1,1]{2,1,0:T(2,128)(2,1)} %copy.20), calls=%async_computation | async-start | bytes 4096 | tf_op jit(solution)/shard_map/all_to_all | solution.py:39
  37.1 3.7 %copy-start = (s32[1,1,16]{2,1,0:T(1,128)S(1)}, s32[1,1,16]{2,1,0:T(1,128)}, u32[]{:S(2)}) copy-start(s32[1,1,16]{2,1,0:T(1,128)} %param.10) | copy-start | bytes 196
  41.9 10.9 %all-to-all-start.1 = ((bf16[4,32,512]{2,1,0:T(8,128)(2,1)}), bf16[4,32,512]{2,1,0:T(8,128)(2,1)S(1)}, u32[]{:S(2)}, u32[]{:S(2)}) async-start(bf16[4,32,512]{2,1,0:T(8,128)(2,1)} %copy.24), calls=%async_computation.1 | async-start | bytes 262144 | tf_op jit(solution)/shard_map/all_to_all | solution.py:38
Sparse Core Ops, SparseCore 0:
  9.2 26.0 all-gather.2
where the time goes:
time: 64.6 us; the launch traced here: 64.2 us
  waiting for transfers between devices  25.2 us (39%)
  between operations  13.5 us (21%)
  starting transfers between devices  11 us (17%)
  matrix products  7.44 us (12%)
  local copies, waits for them, and re-layouts  4.21 us (7%)
  other arithmetic  2.98 us (5%)
    all_gather x1, waiting for transfers between devices, on_device(): every = lax.all_gather(amplitudes[None], 'virt', axis=0, tiled=True)  18.3 us
    all_to_all x1, starting transfers between devices, on_device(): lax.all_to_all(output_marker, 'occ', split_axis=0, concat_axis=0, tiled=T...  6.35 us
    all_to_all x1, waiting for transfers between devices, on_device(): lax.all_to_all(outgoing, 'occ', split_axis=0, concat_axis=0, tiled=True)  6.18 us
    all_to_all x1, starting transfers between devices, on_device(): lax.all_to_all(outgoing, 'occ', split_axis=0, concat_axis=0, tiled=True)  4.6 us
    dot_general x1, matrix products, on_device(): jnp.dot(left, inter, preferred_element_type=jnp.float32)  3.65 us
    dot_general x1, matrix products, on_device(): jnp.dot(chosen_entries, integrals, preferred_element_type=jnp.float32)  2.93 us
    gather x1, local copies, waits for them, and re-layouts, on_device(): chosen_entries = jnp.take(every, panel_owner[0], axis=0)  1.79 us
  transfers between devices with their start and end apart: 3, of which 2 were waited for; matrix products, arithmetic and copies ran while one was open for 16% of the time, Pallas kernels for 0%

commit v1 on v0

--- a/solution.py
+++ b/solution.py
@@ -15,7 +15,12 @@
     n_occ = lax.axis_size("occ")
     half_splits = op_rows // SROWS
     col_tiles = cols // tile
-    every = lax.all_gather(amplitudes[None], "virt", axis=0, tiled=True)
+    ring = [amplitudes[None]]
+    for hop in range(7):
+        ring.append(lax.ppermute(ring[-1], "virt", [(dev, (dev + 1) % 8) for dev in range(8)]))
+    every = jnp.roll(
+        jnp.concatenate(ring[::-1], axis=0), (lax.axis_index("virt") + 1) * ring[0].shape[0], axis=0
+    )
     chosen_entries = jnp.take(every, panel_owner[0], axis=0)
     chosen_entries = chosen_entries.transpose(1, 0, 2).reshape(op_rows, steps * tile)
     accum = jnp.dot(chosen_entries, integrals, preferred_element_type=jnp.float32)

time: 64.6 us -> 61.8 us (0.957)
  between operations: 13.5 us -> 0.23 us
  waiting for transfers between devices: 25.2 us -> 35.3 us
    ppermute x0 -> x7, waiting for transfers between devices: none -> 29.5 us  [on_device(): lax.ppermute(ring[-1], 'virt', [(dev, (dev + 1) % 8) for dev in range(8)])]
    all_gather x1 -> x0, waiting for transfers between devices: 18.3 us -> none  [on_device(): every = lax.all_gather(amplitudes[None], 'virt', axis=0, tiled=True)]
    unnamed x3 -> x20, local copies, waits for them, and re-layouts: 0.11 us -> 1.34 us
    gather x1, local copies, waits for them, and re-layouts: 1.79 us -> 0.56 us  [on_device(): chosen_entries = jnp.take(every, panel_owner[0], axis=0)]
    all_to_all x1, starting transfers between devices: 6.35 us -> 5.56 us  [on_device(): lax.all_to_all(output_marker, 'occ', split_axis=0, concat_axis=0, tiled=T...]
    unnamed x1 -> x0, waiting for transfers between devices: 0.71 us -> none
  transfers between devices with their start and end apart: 3 -> 9, of which waited for: 2 -> 7; matrix products, arithmetic and copies ran while one was open for 16% -> 16% of each run, Pallas kernels for 0% -> 0%
where the time goes in v1:
time: 61.8 us; the launch traced here: 61.4 us
  waiting for transfers between devices  35.3 us (57%)
  starting transfers between devices  11.2 us (18%)
  matrix products  7.44 us (12%)
  local copies, waits for them, and re-layouts  4.31 us (7%)
  other arithmetic  2.98 us (5%)
    ppermute x7, waiting for transfers between devices, on_device(): lax.ppermute(ring[-1], 'virt', [(dev, (dev + 1) % 8) for dev in range(8)])  29.5 us
    all_to_all x1, waiting for transfers between devices, on_device(): lax.all_to_all(outgoing, 'occ', split_axis=0, concat_axis=0, tiled=True)  5.8 us
    all_to_all x1, starting transfers between devices, on_device(): lax.all_to_all(output_marker, 'occ', split_axis=0, concat_axis=0, tiled=T...  5.56 us
    all_to_all x1, starting transfers between devices, on_device(): lax.all_to_all(outgoing, 'occ', split_axis=0, concat_axis=0, tiled=True)  5.09 us
    dot_general x1, matrix products, on_device(): jnp.dot(left, inter, preferred_element_type=jnp.float32)  3.66 us
    dot_general x1, matrix products, on_device(): jnp.dot(chosen_entries, integrals, preferred_element_type=jnp.float32)  2.93 us
    unnamed x20, local copies, waits for them, and re-layouts  1.34 us
  transfers between devices with their start and end apart: 9, of which 7 were waited for; matrix products, arithmetic and copies ran while one was open for 16% of the time, Pallas kernels for 0%

profile of v1, /device:TPU:0, one launch (start us, length us, event | category | flops | bytes accessed | tf_op | source)
XLA Modules:
  0.0 61.4 jit_solution(15775541953678191858)
XLA Ops:
  0.0 0.5 collective-permute-start
  0.5 5.8 %collective-permute-done = bf16[1,128,512]{2,1,0:T(8,128)(2,1)S(1)} collective-permute-done((bf16[1,128,512]{2,1,0:T(8,128)(2,1)}, bf16[1,128,512]{2,1,0:T(8,128)(2,1)S(1)}, u32[]{:S(2)}, u32[]{:S(2)}) %collective-permute-start) | collective-permute-done | bytes 131104 | tf_op jit(solution)/shard_map/ppermute | solution.py:20
  6.3 5.3 %collective-permute-done.1 = bf16[1,128,512]{2,1,0:T(8,128)(2,1)S(1)} collective-permute-done((bf16[1,128,512]{2,1,0:T(8,128)(2,1)S(1)}, bf16[1,128,512]{2,1,0:T(8,128)(2,1)S(1)}, u32[]{:S(2)}, u32[]{:S(2)}) %collective-permute-start.1) | collective-permute-done | bytes 131104 | tf_op jit(solution)/shard_map/ppermute | solution.py:20
  11.6 0.7 %compare_bitcast_fusion = pred[16]{0:T(512)(128)(4,1)S(1)} fusion(s32[1,1,16]{2,1,0:T(1,128)} %param.11), kind=kLoop, calls=%fused_computation.35 | loop fusion | flops 16 | bytes 80 | tf_op jit(solution)/shard_map/eq | solution.py:35
  12.3 4.6 %collective-permute-done.2 = bf16[1,128,512]{2,1,0:T(8,128)(2,1)S(1)} collective-permute-done((bf16[1,128,512]{2,1,0:T(8,128)(2,1)S(1)}, bf16[1,128,512]{2,1,0:T(8,128)(2,1)S(1)}, u32[]{:S(2)}, u32[]{:S(2)}) %collective-permute-start.2) | collective-permute-done | bytes 131104 | tf_op jit(solution)/shard_map/ppermute | solution.py:20
  16.9 0.8 %select_reduce_fusion = s32[4]{0:T(128)S(1)} fusion(s32[16]{0:T(128)S(1)} %iota_add_fusion, s32[16]{0:T(128)} %bitcast.41, pred[16]{0:T(512)(128)(4,1)S(1)} %compare_bitcast_fusion), kind=kLoop, calls=%fused_computation.28 | loop fusion | flops 252 | bytes 160 | tf_op jit(solution)/shard_map/reduce_sum | solution.py:39
  17.7 4.5 %collective-permute-done.3 = bf16[1,128,512]{2,1,0:T(8,128)(2,1)S(1)} collective-permute-done((bf16[1,128,512]{2,1,0:T(8,128)(2,1)S(1)}, bf16[1,128,512]{2,1,0:T(8,128)(2,1)S(1)}, u32[]{:S(2)}, u32[]{:S(2)}) %collective-permute-start.3) | collective-permute-done | bytes 131104 | tf_op jit(solution)/shard_map/ppermute | solution.py:20
  22.2 0.7 %copy.20 = bf16[4,1,1]{2,1,0:T(2,128)(2,1)} copy(bf16[4,1,1]{0,2,1:T(2,128)(2,1)S(1)} %convert_bitcast_fusion) | data formatting | bytes 16 | tf_op jit(solution)/shard_map/convert_element_type | solution.py:39
  22.9 5.6 %all-to-all-start = ((bf16[4,1,1]{2,1,0:T(2,128)(2,1)}), bf16[4,1,1]{2,1,0:T(2,128)(2,1)S(1)}, u32[]{:S(2)}, u32[]{:S(2)}) async-start(bf16[4,1,1]{2,1,0:T(2,128)(2,1)} %copy.20), calls=%async_computation | async-start | bytes 4096 | tf_op jit(solution)/shard_map/all_to_all | solution.py:44
  28.4 0.7 %fusion.11 = s32[2]{0:T(128)S(1)} fusion(s32[1,2]{1,0:T(1,128)} %param.8), kind=kLoop, calls=%fused_computation.40 | loop fusion | flops 6 | bytes 16 | tf_op jit(solution)/shard_map/jit(_take)/jit(_where)/select_n | solution.py:24
  29.1 4.6 %collective-permute-done.5 = bf16[1,128,512]{2,1,0:T(8,128)(2,1)S(1)} collective-permute-done((bf16[1,128,512]{2,1,0:T(8,128)(2,1)S(1)}, bf16[1,128,512]{2,1,0:T(8,128)(2,1)S(1)}, u32[]{:S(2)}, u32[]{:S(2)}) %collective-permute-start.5) | collective-permute-done | bytes 131104 | tf_op jit(solution)/shard_map/ppermute | solution.py:20
  33.7 0.7 %compare_and_fusion = pred[2]{0:T(512)(128)(4,1)S(1)} fusion(s32[1,2]{1,0:T(1,128)} %param.8), kind=kLoop, calls=%fused_computation.33 | loop fusion | flops 12 | bytes 10 | tf_op jit(solution)/shard_map/jit(_take)/and | solution.py:24
  34.4 4.6 %collective-permute-done.6 = bf16[1,128,512]{2,1,0:T(8,128)(2,1)S(1)} collective-permute-done((bf16[1,128,512]{2,1,0:T(8,128)(2,1)S(1)}, bf16[1,128,512]{2,1,0:T(8,128)(2,1)S(1)}, u32[]{:S(2)}, u32[]{:S(2)}) %collective-permute-start.6) | collective-permute-done | bytes 131104 | tf_op jit(solution)/shard_map/ppermute | solution.py:20
  39.1 0.9 %constant_dynamic-update-slice_fusion.8 = bf16[16,128,512]{2,1,0:T(8,128)(2,1)S(1)} fusion(bf16[16,128,512]{2,1,0:T(8,128)(2,1)S(1)} %constant_dynamic-update-slice_fusion.9, bf16[128,512]{1,0:T(8,128)(2,1)} %param.6), kind=kLoop, calls=%fused_computation.16 | loop fusion | bytes 262144
  40.3 0.6 gather_fusion
  41.2 2.9 %convolution_convert_fusion = bf16[128,2048]{1,0:T(8,128)(2,1)S(1)} fusion(bf16[128,1024]{0,1:T(8,128)(2,1)S(1)} %bitcast.39, bf16[1024,2048]{1,0:T(8,128)(2,1)} %param.7), kind=kOutput, calls=%fused_computation.1 | convolution fusion | flops 537133056 | bytes 4980736 | tf_op jit(solution)/shard_map/dot_general | solution.py:26
  44.1 0.4 reshape.88
  44.8 0.4 convolution_convert_fusion.3
  45.2 0.7 %copy.24 = bf16[4,32,512]{2,1,0:T(8,128)(2,1)} copy(bf16[4,32,512]{2,0,1:T(4,128)(2,1)S(1)} %convolution_convert_fusion.3) | data formatting | bytes 262144 | tf_op jit(solution)/shard_map/convert_element_type | solution.py:38
  45.8 5.1 %all-to-all-start.1 = ((bf16[4,32,512]{2,1,0:T(8,128)(2,1)}), bf16[4,32,512]{2,1,0:T(8,128)(2,1)S(1)}, u32[]{:S(2)}, u32[]{:S(2)}) async-start(bf16[4,32,512]{2,1,0:T(8,128)(2,1)} %copy.24), calls=%async_computation.1 | async-start | bytes 262144 | tf_op jit(solution)/shard_map/all_to_all | solution.py:43
  51.1 5.8 %all-to-all-done.1 = bf16[4,32,512]{2,1,0:T(8,128)(2,1)S(1)} async-done(((bf16[4,32,512]{2,1,0:T(8,128)(2,1)}), bf16[4,32,512]{2,1,0:T(8,128)(2,1)S(1)}, u32[]{:S(2)}, u32[]{:S(2)}) %all-to-all-start.1) | async-done | bytes 131104 | tf_op jit(solution)/shard_map/all_to_all | solution.py:43
  56.9 0.5 convolution_convert_fusion.1
  57.4 0.2 copy.26
  57.7 3.7 %convolution_convert_fusion.2 = bf16[128,1024]{1,0:T(8,128)(2,1)} fusion(bf16[128,2048]{1,0:T(8,128)(2,1)S(1)} %bitcast.36, bf16[2048,1024]{1,0:T(8,128)(2,1)} %param.9), kind=kOutput, calls=%fused_computation.3 | convolution fusion | flops 537001984 | bytes 4980736 | tf_op jit(solution)/shard_map/dot_general | solution.py:59
  (38 shorter events, 1.1 us)
Async XLA Ops:
  0.0 40.2 %copy-start = (bf16[128,512]{1,0:T(8,128)(2,1)S(1)}, bf16[128,512]{1,0:T(8,128)(2,1)}, u32[]{:S(2)}) copy-start(bf16[128,512]{1,0:T(8,128)(2,1)} %param.6) | copy-start | bytes 393220
  0.0 6.3 %collective-permute-start = (bf16[1,128,512]{2,1,0:T(8,128)(2,1)}, bf16[1,128,512]{2,1,0:T(8,128)(2,1)S(1)}, u32[]{:S(2)}, u32[]{:S(2)}) collective-permute-start(bf16[1,128,512]{2,1,0:T(8,128)(2,1)} %bitcast.40), channel_id=1, source_target_pairs={{0,4},{4,8},{8,12},{12,16},{16,20},{20,24},{24,28},{28,0},{1,5},{5... | collective-permute-start | bytes 393224 | tf_op jit(solution)/shard_map/ppermute | solution.py:20
  6.3 5.3 %collective-permute-start.1 = (bf16[1,128,512]{2,1,0:T(8,128)(2,1)S(1)}, bf16[1,128,512]{2,1,0:T(8,128)(2,1)S(1)}, u32[]{:S(2)}, u32[]{:S(2)}) collective-permute-start(bf16[1,128,512]{2,1,0:T(8,128)(2,1)S(1)} %collective-permute-done), channel_id=1, source_target_pairs={{0,4},{4,8},{8,12},{12,16},{16,20},{20,24},{24,28},{28,0},{1,5},{5... | collective-permute-start | bytes 393224 | tf_op jit(solution)/shard_map/ppermute | solution.py:20
  11.6 5.3 %collective-permute-start.2 = (bf16[1,128,512]{2,1,0:T(8,128)(2,1)S(1)}, bf16[1,128,512]{2,1,0:T(8,128)(2,1)S(1)}, u32[]{:S(2)}, u32[]{:S(2)}) collective-permute-start(bf16[1,128,512]{2,1,0:T(8,128)(2,1)S(1)} %collective-permute-done.1), channel_id=1, source_target_pairs={{0,4},{4,8},{8,12},{12,16},{16,20},{20,24},{24,28},{28,0},{1,5},{5... | collective-permute-start | bytes 393224 | tf_op jit(solution)/shard_map/ppermute | solution.py:20
  16.9 5.3 %collective-permute-start.3 = (bf16[1,128,512]{2,1,0:T(8,128)(2,1)S(1)}, bf16[1,128,512]{2,1,0:T(8,128)(2,1)S(1)}, u32[]{:S(2)}, u32[]{:S(2)}) collective-permute-start(bf16[1,128,512]{2,1,0:T(8,128)(2,1)S(1)} %collective-permute-done.2), channel_id=1, source_target_pairs={{0,4},{4,8},{8,12},{12,16},{16,20},{20,24},{24,28},{28,0},{1,5},{5... | collective-permute-start | bytes 393224 | tf_op jit(solution)/shard_map/ppermute | solution.py:20
  22.2 6.3 %collective-permute-start.4 = (bf16[1,128,512]{2,1,0:T(8,128)(2,1)S(1)}, bf16[1,128,512]{2,1,0:T(8,128)(2,1)S(1)}, u32[]{:S(2)}, u32[]{:S(2)}) collective-permute-start(bf16[1,128,512]{2,1,0:T(8,128)(2,1)S(1)} %collective-permute-done.3), channel_id=1, source_target_pairs={{0,4},{4,8},{8,12},{12,16},{16,20},{20,24},{24,28},{28,0},{1,5},{5... | collective-permute-start | bytes 393224 | tf_op jit(solution)/shard_map/ppermute | solution.py:20
  22.9 23.0 %all-to-all-start = ((bf16[4,1,1]{2,1,0:T(2,128)(2,1)}), bf16[4,1,1]{2,1,0:T(2,128)(2,1)S(1)}, u32[]{:S(2)}, u32[]{:S(2)}) async-start(bf16[4,1,1]{2,1,0:T(2,128)(2,1)} %copy.20), calls=%async_computation | async-start | bytes 4096 | tf_op jit(solution)/shard_map/all_to_all | solution.py:44
  28.4 5.3 %collective-permute-start.5 = (bf16[1,128,512]{2,1,0:T(8,128)(2,1)S(1)}, bf16[1,128,512]{2,1,0:T(8,128)(2,1)S(1)}, u32[]{:S(2)}, u32[]{:S(2)}) collective-permute-start(bf16[1,128,512]{2,1,0:T(8,128)(2,1)S(1)} %collective-permute-done.4), channel_id=1, source_target_pairs={{0,4},{4,8},{8,12},{12,16},{16,20},{20,24},{24,28},{28,0},{1,5},{5... | collective-permute-start | bytes 393224 | tf_op jit(solution)/shard_map/ppermute | solution.py:20
  33.7 5.3 %collective-permute-start.6 = (bf16[1,128,512]{2,1,0:T(8,128)(2,1)S(1)}, bf16[1,128,512]{2,1,0:T(8,128)(2,1)S(1)}, u32[]{:S(2)}, u32[]{:S(2)}) collective-permute-start(bf16[1,128,512]{2,1,0:T(8,128)(2,1)S(1)} %collective-permute-done.5), channel_id=1, source_target_pairs={{0,4},{4,8},{8,12},{12,16},{16,20},{20,24},{24,28},{28,0},{1,5},{5... | collective-permute-start | bytes 393224 | tf_op jit(solution)/shard_map/ppermute | solution.py:20
  44.1 0.7 %copy-start.1 = (s32[1,1,16]{2,1,0:T(1,128)S(1)}, s32[1,1,16]{2,1,0:T(1,128)}, u32[]{:S(2)}) copy-start(s32[1,1,16]{2,1,0:T(1,128)} %param.10) | copy-start | bytes 196
  45.8 11.0 %all-to-all-start.1 = ((bf16[4,32,512]{2,1,0:T(8,128)(2,1)}), bf16[4,32,512]{2,1,0:T(8,128)(2,1)S(1)}, u32[]{:S(2)}, u32[]{:S(2)}) async-start(bf16[4,32,512]{2,1,0:T(8,128)(2,1)} %copy.24), calls=%async_computation.1 | async-start | bytes 262144 | tf_op jit(solution)/shard_map/all_to_all | solution.py:43
